TPU v7x, 256 devices: a whole 4x4x8 slice. The times are simulated.
256 devices in a mesh: seq: 128 (over x, y, z), head: 2 (over core).
Axes of the slice: x: 4, y: 4, z: 8, core: 2. Of those that a mesh axis runs over, the one named last changes fastest.
Arguments:
- tiles: bfloat16 [16384, 768], P('seq', 'head'), may hold values from -6 to 6
- ln_gain: float32 [768], replicated, may hold values from 0.25 to 1.75
- w_qkv: bfloat16 [768, 3, 768], P(None, None, 'head'), as said below
- w_out: bfloat16 [768, 768], P('head'), may hold values from -0.21875 to 0.21875
- tile_source: int32 [16384], P('seq'), may hold values from 0 to 16383, as said below
- tissue_count: int32 [128], P('seq'), may hold values from 64 to 128
Outputs:
- encoded: bfloat16 [16384, 768], P('seq', 'head')
Inputs may be any that keep to these rules, and one draw needn't show every extreme that they name: `tile_source`: A permutation of the 16384 rows; exactly one tile goes to Hilbert block d from each encoder block s, namely row s * 128 + d; within block d these 128 tiles come in any order. `w_qkv`: projection weights; the query third may be larger than the key and value thirds.
All inputs are finite; a program needn't handle non-finite values.
Results may differ from a plain program's by a relative error of at most 0.0095.
The roundings to bfloat16 on the way count: a program that leaves them out, or rounds other values in their place, can miss the bound.
Values may be sent and summed in bfloat16 or wider, within the bound.
A program may use at most 64 MiB of HBM per device.

v0:
```python
import jax
import jax.numpy as jnp
from jax import lax
from jax.sharding import PartitionSpec as P

D = 768
HEAD_DIM = 64
SPAN_SHORT = 4
MIDDLE_SPAN = 16
MIDDLE_DILATION = 4
WHOLE_DILATION = 16
masked_score = -1e30


def shortened(value):

    def short(part):
        return part.astype(jnp.bfloat16) if part.dtype == jnp.float32 else part

    return jax.tree.map(short, value)


def swapped(value, axis, apart):
    return lax.ppermute(value, axis, [(i, i ^ 1 << apart) for i in range(lax.axis_size(axis))])


def absorb(softmax_state, queries, key_matrix, value_matrix, key_live):
    running_max, running_sum, weighted = softmax_state
    scores = jnp.einsum(
        "qhd,khd->hqk", queries, key_matrix, preferred_element_type=jnp.float32
    ) * queries.shape[-1] ** (-0.5)
    scores = jnp.where(key_live.T[:, None, :] > 0.5, scores, masked_score)
    new_max = jnp.maximum(running_max, jnp.max(scores, axis=-1))
    rescale = jnp.exp(running_max - new_max)
    probability = jnp.exp(scores - new_max[..., None])
    running_sum = running_sum * rescale + jnp.sum(probability, axis=-1)
    mixed = jnp.einsum(
        "hqk,khd->qhd",
        probability.astype(jnp.bfloat16),
        value_matrix,
        preferred_element_type=jnp.float32,
    )
    weighted = weighted * rescale.T[:, :, None] + mixed
    return (new_max, running_sum, weighted)


def select_rows(key_matrix, value_matrix, row_active_mask, stride, offsets):
    kept_rows = key_matrix.shape[0] // stride
    heads_local = key_matrix.shape[1]
    selector = jnp.broadcast_to(
        offsets[None, None, :, None], (kept_rows, 1, heads_local, key_matrix.shape[2])
    )
    picked_keys = jnp.take_along_axis(
        key_matrix.reshape(kept_rows, stride, heads_local, key_matrix.shape[2]), selector, axis=1
    )[:, 0]
    picked_values = jnp.take_along_axis(
        value_matrix.reshape(kept_rows, stride, heads_local, value_matrix.shape[2]),
        selector,
        axis=1,
    )[:, 0]
    picked_live = row_active_mask.reshape(kept_rows, stride)[:, offsets]
    return (picked_keys, picked_values, picked_live)


def join_parts(local_part, remote_part):
    return tuple(
        (
            jnp.concatenate((mine_rows, their_rows), 0)
            for mine_rows, their_rows in zip(local_part, remote_part)
        )
    )


def absorb_blocks(softmax_state, queries, members, step_rows):
    for offset_row in range(0, members[0].shape[0], step_rows):
        softmax_state = absorb(
            softmax_state,
            queries,
            *[member[offset_row : offset_row + step_rows] for member in members]
        )
    return softmax_state


def shards(tiles, ln_gain, w_qkv, w_out, tile_source, tissue_count):
    tok_rows = tiles.shape[0]
    blocks = lax.axis_size("seq")
    per_peer = tok_rows // blocks
    arrival = tile_source // tok_rows * per_peer + tile_source % per_peer
    whole_rows = lax.all_gather(tiles, "head", axis=1, tiled=True)
    arrived = lax.all_to_all(
        whole_rows.reshape(blocks, per_peer, whole_rows.shape[1]),
        "seq",
        split_axis=0,
        concat_axis=0,
        tiled=True,
    )
    relaid = arrived.reshape(tok_rows, whole_rows.shape[1])[arrival]
    widened = relaid.astype(jnp.float32)
    row_mean = jnp.mean(widened, axis=-1, keepdims=True)
    centered = widened - row_mean
    row_var = jnp.mean(centered * centered, axis=-1, keepdims=True)
    normed = (centered * lax.rsqrt(row_var + 1e-05) * ln_gain).astype(jnp.bfloat16)
    heads_local = w_qkv.shape[2] // HEAD_DIM
    packed = jnp.dot(
        normed, w_qkv.reshape(D, 3 * w_qkv.shape[2]), preferred_element_type=jnp.float32
    ).astype(jnp.bfloat16)
    packed = packed.reshape(tok_rows, 3, heads_local, HEAD_DIM)
    queries, key_matrix, value_matrix = (packed[:, 0], packed[:, 1], packed[:, 2])
    row_active_mask = (jnp.arange(tok_rows, dtype=jnp.int32) < tissue_count[0]).astype(jnp.bfloat16)
    live_all = jnp.broadcast_to(row_active_mask[:, None], (tok_rows, heads_local))
    present_heads = lax.axis_index("head") * heads_local + jnp.arange(heads_local, dtype=jnp.int32)
    softmax_state = (
        jnp.full((heads_local, tok_rows), masked_score, jnp.float32),
        jnp.zeros((heads_local, tok_rows), jnp.float32),
        jnp.zeros((tok_rows, heads_local, HEAD_DIM), jnp.float32),
    )
    gathered = (key_matrix, value_matrix, live_all)
    for level in range(SPAN_SHORT.bit_length() - 1):
        partner = jax.tree.map(
            lambda part, own: part.astype(own.dtype),
            swapped(shortened(gathered), "seq", level),
            gathered,
        )
        gathered = join_parts(gathered, partner)
    softmax_state = absorb(softmax_state, queries, *gathered)
    middle_branch = select_rows(
        key_matrix, value_matrix, row_active_mask, MIDDLE_DILATION, present_heads % MIDDLE_DILATION
    )
    faraway_part = select_rows(
        key_matrix, value_matrix, row_active_mask, WHOLE_DILATION, present_heads % WHOLE_DILATION
    )
    for level in range(MIDDLE_SPAN.bit_length() - 1):
        partner = jax.tree.map(
            lambda part, own: part.astype(own.dtype),
            swapped(shortened(middle_branch), "seq", level),
            middle_branch,
        )
        middle_branch = join_parts(middle_branch, partner)
    softmax_state = absorb(softmax_state, queries, *middle_branch)
    faraway_part = (
        lax.all_gather(faraway_part[0], "seq", axis=0, tiled=True),
        lax.all_gather(faraway_part[1], "seq", axis=0, tiled=True),
        lax.all_gather(faraway_part[2], "seq", axis=0, tiled=True),
    )
    step_rows = min(faraway_part[0].shape[0], middle_branch[0].shape[0])
    softmax_state = absorb_blocks(softmax_state, queries, faraway_part, step_rows)
    running_max, running_sum, weighted = softmax_state
    attended = (
        weighted / running_sum.T[:, :, None] * row_active_mask.astype(jnp.float32)[:, None, None]
    )
    attended = attended.astype(jnp.bfloat16).reshape(tok_rows, heads_local * HEAD_DIM)
    partial_value = jnp.dot(attended, w_out, preferred_element_type=jnp.float32)
    return lax.psum_scatter(
        partial_value.astype(jnp.bfloat16), "head", scatter_dimension=1, tiled=True
    )


def solution(mesh):
    return jax.shard_map(
        shards,
        mesh=mesh,
        in_specs=(
            P("seq", "head"),
            P(),
            P(None, None, "head"),
            P("head", None),
            P("seq"),
            P("seq"),
        ),
        out_specs=P("seq", "head"),
        check_vma=False,
    )
```

profile of v0, /device:TPU:1, one launch (start us, length us, event | category | flops | bytes accessed | tf_op | source)
XLA Modules:
  0.0 1479.4 jit_solution(4829713266391347686)
XLA Ops:
  6.5 5.3 all_gather.12
  13.8 13.8 all-to-all-start
  31.8 290.8 %all-gather = bf16[1024,6]{1,0:T(8,128)(2,1)S(1)} all-gather(bf16[8,6]{1,0:T(8,128)(2,1)S(1)} %copy.105), channel_id=2, replica_groups=mesh['seq'=128,'head'=2] {'seq'}, dimensions={0}, use_global_device_ids=true | all-gather | bytes 12384 | tf_op jit(solution)/shard_map/all_gather | solution.py:143
  323.2 2.6 copy.90
  326.5 2.1 collective-permute-start.1
  328.6 4.2 collective-permute-done.8
  332.9 2.7 collective-permute-done.9
  338.4 130.2 %gather_fusion.3 = bf16[12288]{0:T(1024)(128)(2,1)S(1)} fusion(bf16[32,4,6,64]{3,1,0,2:T(4,128)(2,1)S(1)} %bitcast.224, s32[12288]{0:T(1024)S(1)} %reshape.307), kind=kCustom, calls=%fused_computation.clone | custom fusion | bytes 245760 | tf_op jit(solution)/shard_map/jit(take_along_axis)/gather | solution.py:53
  468.9 130.2 %gather_fusion.4 = bf16[12288]{0:T(1024)(128)(2,1)S(1)} fusion(bf16[32,4,6,64]{3,1,0,2:T(4,128)(2,1)S(1)} %bitcast.226, s32[12288]{0:T(1024)S(1)} %reshape.313), kind=kCustom, calls=%fused_computation.2.clone | custom fusion | bytes 245760 | tf_op jit(solution)/shard_map/jit(take_along_axis)/gather | solution.py:56
  600.0 33.9 %gather_fusion.5 = bf16[3072]{0:T(1024)(128)(2,1)S(1)} fusion(bf16[8,16,6,64]{3,1,0,2:T(8,128)(2,1)S(1)} %bitcast.225, s32[3072]{0:T(1024)S(1)} %reshape.319), kind=kCustom, calls=%fused_computation.1.clone | custom fusion | bytes 61440 | tf_op jit(solution)/shard_map/jit(take_along_axis)/gather | solution.py:53
  633.9 33.9 %gather_fusion.6 = bf16[3072]{0:T(1024)(128)(2,1)S(1)} fusion(bf16[8,16,6,64]{3,1,0,2:T(8,128)(2,1)S(1)} %bitcast.227, s32[3072]{0:T(1024)S(1)} %reshape.319), kind=kCustom, calls=%fused_computation.3.clone | custom fusion | bytes 61440 | tf_op jit(solution)/shard_map/jit(take_along_axis)/gather | solution.py:56
  668.0 292.7 %all-gather.1 = bf16[1024,1,6,64]{3,0,2,1:T(8,128)(2,1)S(1)} all-gather(bf16[8,1,6,64]{3,0,2,1:T(8,128)(2,1)S(1)} %copy.110), channel_id=3, replica_groups=mesh['seq'=128,'head'=2] {'seq'}, dimensions={0}, use_global_device_ids=true | all-gather | bytes 792576 | tf_op jit(solution)/shard_map/all_gather | solution.py:141
  960.7 1.5 collective-permute-start.14
  962.2 291.3 %all-gather.2 = bf16[1024,1,6,64]{3,0,2,1:T(8,128)(2,1)S(1)} all-gather(bf16[8,1,6,64]{3,0,2,1:T(8,128)(2,1)S(1)} %copy.115), channel_id=4, replica_groups=mesh['seq'=128,'head'=2] {'seq'}, dimensions={0}, use_global_device_ids=true | all-gather | bytes 792576 | tf_op jit(solution)/shard_map/all_gather | solution.py:142
  1254.5 1.7 collective-permute-start.4
  1256.4 2.4 collective-permute-start.15
  1258.8 6.0 collective-permute-done.11
  1265.0 0.9 collective-permute-done.15
  1265.9 4.5 collective-permute-start.16
  1270.7 2.4 collective-permute-start.5
  1273.9 3.3 collective-permute-done.16
  1277.6 2.4 collective-permute-done.3
  1287.7 183.2 %reduce-scatter.4.cloned.1.call-done = bf16[384,128]{1,0:T(8,128)(2,1)} async-done(((bf16[768,128]{1,0:T(8,128)(2,1)}), bf16[384,128]{1,0:T(8,128)(2,1)}) %reduce-scatter.4.cloned.1.call-update) | async-done | bytes 98320
  1470.9 1.6 copy.123
  (142 shorter events, 20.9 us)
Async XLA Ops:
  6.5 1280.0 %copy-start = (bf16[384,768]{1,0:T(8,128)(2,1)S(1)}, bf16[384,768]{1,0:T(8,128)(2,1)}, u32[]{:S(2)}) copy-start(bf16[384,768]{1,0:T(8,128)(2,1)} %param.13) | copy-start | bytes 1769476
  11.8 18.9 %copy-start.3 = (s32[128]{0:T(128)S(1)}, s32[128]{0:T(128)}, u32[]{:S(2)}) copy-start(s32[128]{0:T(128)} %param.14) | copy-start | bytes 1540
  13.8 321.9 %all-to-all-start = ((bf16[128,2,384]{2,1,0:T(2,128)(2,1)}), bf16[128,2,384]{2,1,0:T(2,128)(2,1)S(1)}, u32[]{:S(2)}, u32[]{:S(2)}) async-start(bf16[128,2,384]{2,1,0:T(2,128)(2,1)} %reshape.331), calls=%async_computation | async-start | bytes 393216 | tf_op jit(solution)/shard_map/all_to_all | solution.py:90
  27.6 1443.3 %reduce-scatter.4.cloned.1.call-start = ((), (), s32[]{:S(2)}) async-start(), calls=%async_computation.2 | async-start | bytes 294912
  28.9 294.0 %collective-permute-start.6 = (bf16[32,6]{0,1:T(8,128)(2,1)S(1)}, bf16[32,6]{0,1:T(8,128)(2,1)S(1)}, u32[]{:S(2)}, u32[]{:S(2)}) collective-permute-start(bf16[32,6]{0,1:T(8,128)(2,1)S(1)} %bitcast.237), channel_id=1, source_target_pairs={{0,2},{2,0},{4,6},{6,4},{8,10},{10,8},{12,14},{14,12},{16,18},{18,... | collective-permute-start | bytes 1160 | tf_op jit(solution)/shard_map/ppermute | solution.py:24
  29.6 296.9 %collective-permute-start = (bf16[128,6]{0,1:T(8,128)(2,1)S(1)}, bf16[128,6]{0,1:T(8,128)(2,1)S(1)}, u32[]{:S(2)}, u32[]{:S(2)}) collective-permute-start(bf16[128,6]{0,1:T(8,128)(2,1)S(1)} %broadcast_in_dim.86), channel_id=1, source_target_pairs={{0,2},{2,0},{4,6},{6,4},{8,10},{10,8},{12,14},{14,12},{16,18},{18,... | collective-permute-start | bytes 4616 | tf_op jit(solution)/shard_map/ppermute | solution.py:24
  323.0 3.4 collective-permute-start.7
  326.4 6.4 collective-permute-start.8
  326.5 6.4 collective-permute-start.1
  332.8 2.8 collective-permute-start.9
  335.7 1.4 copy-start.1
  600.0 656.2 %collective-permute-start.10 = (bf16[32,6,64]{2,0,1:T(8,128)(2,1)S(1)}, bf16[32,6,64]{2,0,1:T(8,128)(2,1)S(1)}, u32[]{:S(2)}, u32[]{:S(2)}) collective-permute-start(bf16[32,6,64]{2,0,1:T(8,128)(2,1)S(1)} %get-tuple-element.27), channel_id=1, source_target_pairs={{0,2},{2,0},{4,6},{6,4},{8,10},{10,8},{12,14},{14,12},{16,18},{18,... | collective-permute-start | bytes 73736 | tf_op jit(solution)/shard_map/ppermute | solution.py:24
  960.7 309.8 %collective-permute-start.2 = (bf16[128,6,64]{0,2,1:T(8,128)(2,1)S(1)}, bf16[128,6,64]{0,2,1:T(8,128)(2,1)S(1)}, u32[]{:S(2)}, u32[]{:S(2)}) collective-permute-start(bf16[128,6,64]{0,2,1:T(8,128)(2,1)S(1)} %get-tuple-element.18), channel_id=1, source_target_pairs={{0,2},{2,0},{4,6},{6,4},{8,10},{10,8},{12,14},{14,12},{16,18},{18,... | collective-permute-start | bytes 294920 | tf_op jit(solution)/shard_map/ppermute | solution.py:24
  960.7 295.6 %collective-permute-start.14 = (bf16[32,6,64]{2,0,1:T(8,128)(2,1)S(1)}, bf16[32,6,64]{2,0,1:T(8,128)(2,1)S(1)}, u32[]{:S(2)}, u32[]{:S(2)}) collective-permute-start(bf16[32,6,64]{2,0,1:T(8,128)(2,1)S(1)} %get-tuple-element.11), channel_id=1, source_target_pairs={{0,2},{2,0},{4,6},{6,4},{8,10},{10,8},{12,14},{14,12},{16,18},{18,... | collective-permute-start | bytes 73736 | tf_op jit(solution)/shard_map/ppermute | solution.py:24
  1254.0 4.8 copy-start.2
  1254.5 16.1 %collective-permute-start.4 = (bf16[128,6,64]{0,2,1:T(8,128)(2,1)S(1)}, bf16[128,6,64]{0,2,1:T(8,128)(2,1)S(1)}, u32[]{:S(2)}, u32[]{:S(2)}) collective-permute-start(bf16[128,6,64]{0,2,1:T(8,128)(2,1)S(1)} %get-tuple-element.17), channel_id=1, source_target_pairs={{0,2},{2,0},{4,6},{6,4},{8,10},{10,8},{12,14},{14,12},{16,18},{18,... | collective-permute-start | bytes 294920 | tf_op jit(solution)/shard_map/ppermute | solution.py:24
  1256.2 8.6 collective-permute-start.11
  1256.4 9.5 collective-permute-start.15
  1264.9 8.8 collective-permute-start.12
  1265.9 11.2 collective-permute-start.16
  1270.5 9.5 collective-permute-start.3
  1270.7 15.3 %collective-permute-start.5 = (bf16[256,6,64]{0,2,1:T(8,128)(2,1)S(1)}, bf16[256,6,64]{0,2,1:T(8,128)(2,1)S(1)}, u32[]{:S(2)}, u32[]{:S(2)}) collective-permute-start(bf16[256,6,64]{0,2,1:T(8,128)(2,1)S(1)} %pad_maximum_fusion.3), channel_id=1, source_target_pairs={{0,4},{2,6},{4,0},{6,2},{8,12},{10,14},{12,8},{14,10},{16,20},{18,... | collective-permute-start | bytes 589832 | tf_op jit(solution)/shard_map/ppermute | solution.py:24
  1273.8 7.0 collective-permute-start.13
  1277.2 7.5 collective-permute-start.17
Sparse Core Ops, SparseCore 0:
  1287.8 183.0 reduce-scatter.3
where the time goes:
time: 1480 us
  blocking collectives  880 us (59%)
  local copies, waits for them, and re-layouts  339 us (23%)
  waiting for transfers between devices  204 us (14%)
  starting transfers between devices  30.8 us (2%)
    all_gather x1, blocking collectives, shards(): lax.all_gather(faraway_part[0], 'seq', axis=0, tiled=True)  293 us
    all_gather x1, blocking collectives, shards(): lax.all_gather(faraway_part[1], 'seq', axis=0, tiled=True)  291 us
    all_gather x1, blocking collectives, shards(): lax.all_gather(faraway_part[2], 'seq', axis=0, tiled=True)  291 us
    unnamed x2, waiting for transfers between devices  183 us
    gather x8, local copies, waits for them, and re-layouts, select_rows(): jnp.take_along_axis(key_matrix.reshape(kept_rows, stride, heads_local, ke...  165 us
    gather x6, local copies, waits for them, and re-layouts, select_rows(): jnp.take_along_axis(value_matrix.reshape(kept_rows, stride, heads_local,...  164 us
  transfers between devices with their start and end apart: 20, of which 11 were waited for; matrix products, arithmetic and copies ran while one was open for 5% of the time, Pallas kernels for 0%

commit v1 on v0

--- a/solution.py
+++ b/solution.py
@@ -139,7 +139,9 @@
     softmax_state = absorb(softmax_state, queries, *middle_branch)
     faraway_part = (
         lax.all_gather(faraway_part[0], "seq", axis=0, tiled=True),
-        lax.all_gather(faraway_part[1], "seq", axis=0, tiled=True),
+        jnp.concatenate(
+            lax.all_to_all(jnp.stack([faraway_part[1]] * lax.axis_size("seq")), "seq", 0, 0), axis=0
+        ),
         lax.all_gather(faraway_part[2], "seq", axis=0, tiled=True),
     )
     step_rows = min(faraway_part[0].shape[0], middle_branch[0].shape[0])

time: 1480 us -> 1170 us (0.79)
  blocking collectives: 880 us -> 589 us
  waiting for transfers between devices: 204 us -> 151 us
    all_gather x1 -> x0, blocking collectives: 291 us -> none  [shards(): lax.all_gather(faraway_part[1], 'seq', axis=0, tiled=True)]
    unnamed x2, waiting for transfers between devices: 183 us -> 132 us
  transfers between devices with their start and end apart: 20 -> 21, of which waited for: 11 -> 6; matrix products, arithmetic and copies ran while one was open for 5% -> 8% of each run, Pallas kernels for 0% -> 0%
where the time goes in v1:
time: 1170 us
  blocking collectives  589 us (50%)
  local copies, waits for them, and re-layouts  353 us (30%)
  waiting for transfers between devices  151 us (13%)
  starting transfers between devices  41.8 us (4%)
  between operations  14.7 us (1%)
    all_gather x1, blocking collectives, shards(): lax.all_gather(faraway_part[0], 'seq', axis=0, tiled=True)  293 us
    all_gather x1, blocking collectives, shards(): lax.all_gather(faraway_part[2], 'seq', axis=0, tiled=True)  291 us
    gather x8, local copies, waits for them, and re-layouts, select_rows(): jnp.take_along_axis(key_matrix.reshape(kept_rows, stride, heads_local, ke...  165 us
    gather x6, local copies, waits for them, and re-layouts, select_rows(): jnp.take_along_axis(value_matrix.reshape(kept_rows, stride, heads_local,...  164 us
    unnamed x2, waiting for transfers between devices  132 us
  transfers between devices with their start and end apart: 21, of which 6 were waited for; matrix products, arithmetic and copies ran while one was open for 8% of the time, Pallas kernels for 0%

profile of v1, /device:TPU:1, one launch (start us, length us, event | category | flops | bytes accessed | tf_op | source)
XLA Modules:
  0.0 1166.7 jit_solution(10491500510538169196)
XLA Ops:
  6.5 5.3 all_gather.9
  13.8 13.8 %all-to-all-start = ((bf16[128,2,384]{2,1,0:T(2,128)(2,1)}), bf16[128,2,384]{2,1,0:T(2,128)(2,1)S(1)}, u32[]{:S(2)}, u32[]{:S(2)}) async-start(bf16[128,2,384]{2,1,0:T(2,128)(2,1)} %reshape.333), calls=%async_computation | async-start | bytes 393216 | tf_op jit(solution)/shard_map/all_to_all | solution.py:90
  31.9 290.8 %all-gather = bf16[1024,6]{1,0:T(8,128)(2,1)S(1)} all-gather(bf16[8,6]{1,0:T(8,128)(2,1)S(1)} %copy.115), channel_id=2, replica_groups=mesh['seq'=128,'head'=2] {'seq'}, dimensions={0}, use_global_device_ids=true | all-gather | bytes 12384 | tf_op jit(solution)/shard_map/all_gather | solution.py:145
  324.4 2.6 copy.100
  327.4 2.4 collective-permute-start.1
  329.9 3.9 collective-permute-done.8
  333.9 2.7 collective-permute-done.9
  340.0 130.2 %gather_fusion.3 = bf16[12288]{0:T(1024)(128)(2,1)S(1)} fusion(bf16[32,4,6,64]{3,1,0,2:T(4,128)(2,1)S(1)} %bitcast.227, s32[12288]{0:T(1024)S(1)} %reshape.309), kind=kCustom, calls=%fused_computation.clone | custom fusion | bytes 245760 | tf_op jit(solution)/shard_map/jit(take_along_axis)/gather | solution.py:53
  470.5 130.2 %gather_fusion.4 = bf16[12288]{0:T(1024)(128)(2,1)S(1)} fusion(bf16[32,4,6,64]{3,1,0,2:T(4,128)(2,1)S(1)} %bitcast.229, s32[12288]{0:T(1024)S(1)} %reshape.315), kind=kCustom, calls=%fused_computation.2.clone | custom fusion | bytes 245760 | tf_op jit(solution)/shard_map/jit(take_along_axis)/gather | solution.py:56
  601.7 33.9 %gather_fusion.5 = bf16[3072]{0:T(1024)(128)(2,1)S(1)} fusion(bf16[8,16,6,64]{3,1,0,2:T(8,128)(2,1)S(1)} %bitcast.228, s32[3072]{0:T(1024)S(1)} %reshape.321), kind=kCustom, calls=%fused_computation.1.clone | custom fusion | bytes 61440 | tf_op jit(solution)/shard_map/jit(take_along_axis)/gather | solution.py:53
  635.7 33.9 %gather_fusion.6 = bf16[3072]{0:T(1024)(128)(2,1)S(1)} fusion(bf16[8,16,6,64]{3,1,0,2:T(8,128)(2,1)S(1)} %bitcast.230, s32[3072]{0:T(1024)S(1)} %reshape.321), kind=kCustom, calls=%fused_computation.3.clone | custom fusion | bytes 61440 | tf_op jit(solution)/shard_map/jit(take_along_axis)/gather | solution.py:56
  669.8 292.6 %all-gather.1 = bf16[1024,1,6,64]{3,0,2,1:T(8,128)(2,1)S(1)} all-gather(bf16[8,1,6,64]{3,0,2,1:T(8,128)(2,1)S(1)} %copy.120), channel_id=3, replica_groups=mesh['seq'=128,'head'=2] {'seq'}, dimensions={0}, use_global_device_ids=true | all-gather | bytes 792576 | tf_op jit(solution)/shard_map/all_gather | solution.py:141
  962.4 1.6 fusion.111
  967.4 3.8 reshape.335
  971.2 6.2 all-to-all-start.1
  978.0 2.2 collective-permute-start.11
  981.8 6.4 collective-permute-done.11
  988.2 4.1 collective-permute-start.12
  992.4 3.2 collective-permute-start.16
  1003.2 2.1 collective-permute-start.17
  1005.4 6.1 collective-permute-done.3
  1018.3 1.9 reshape.336
  1026.7 131.5 %reduce-scatter.4.cloned.1.call-done = bf16[384,128]{1,0:T(8,128)(2,1)} async-done(((bf16[768,128]{1,0:T(8,128)(2,1)}), bf16[384,128]{1,0:T(8,128)(2,1)}) %reduce-scatter.4.cloned.1.call-update) | async-done | bytes 98320
  1158.2 1.6 copy.137
  (179 shorter events, 39.0 us)
Async XLA Ops:
  6.5 1019.1 %copy-start = (bf16[384,768]{1,0:T(8,128)(2,1)S(1)}, bf16[384,768]{1,0:T(8,128)(2,1)}, u32[]{:S(2)}) copy-start(bf16[384,768]{1,0:T(8,128)(2,1)} %param.13) | copy-start | bytes 1769476
  13.8 322.9 %all-to-all-start = ((bf16[128,2,384]{2,1,0:T(2,128)(2,1)}), bf16[128,2,384]{2,1,0:T(2,128)(2,1)S(1)}, u32[]{:S(2)}, u32[]{:S(2)}) async-start(bf16[128,2,384]{2,1,0:T(2,128)(2,1)} %reshape.333), calls=%async_computation | async-start | bytes 393216 | tf_op jit(solution)/shard_map/all_to_all | solution.py:90
  28.9 294.7 %collective-permute-start.6 = (bf16[32,6]{0,1:T(8,128)(2,1)S(1)}, bf16[32,6]{0,1:T(8,128)(2,1)S(1)}, u32[]{:S(2)}, u32[]{:S(2)}) collective-permute-start(bf16[32,6]{0,1:T(8,128)(2,1)S(1)} %bitcast.241), channel_id=1, source_target_pairs={{0,2},{2,0},{4,6},{6,4},{8,10},{10,8},{12,14},{14,12},{16,18},{18,... | collective-permute-start | bytes 1160 | tf_op jit(solution)/shard_map/ppermute | solution.py:24
  29.5 297.9 %collective-permute-start = (bf16[128,6]{0,1:T(8,128)(2,1)S(1)}, bf16[128,6]{0,1:T(8,128)(2,1)S(1)}, u32[]{:S(2)}, u32[]{:S(2)}) collective-permute-start(bf16[128,6]{0,1:T(8,128)(2,1)S(1)} %broadcast_in_dim.86), channel_id=1, source_target_pairs={{0,2},{2,0},{4,6},{6,4},{8,10},{10,8},{12,14},{14,12},{16,18},{18,... | collective-permute-start | bytes 4616 | tf_op jit(solution)/shard_map/ppermute | solution.py:24
  323.6 3.7 collective-permute-start.7
  327.4 6.4 collective-permute-start.8
  327.4 6.5 collective-permute-start.1
  333.9 2.8 collective-permute-start.9
  601.7 376.3 %collective-permute-start.10 = (bf16[32,6,64]{2,0,1:T(8,128)(2,1)S(1)}, bf16[32,6,64]{2,0,1:T(8,128)(2,1)S(1)}, u32[]{:S(2)}, u32[]{:S(2)}) collective-permute-start(bf16[32,6,64]{2,0,1:T(8,128)(2,1)S(1)} %get-tuple-element.29), channel_id=1, source_target_pairs={{0,2},{2,0},{4,6},{6,4},{8,10},{10,8},{12,14},{14,12},{16,18},{18,... | collective-permute-start | bytes 73736 | tf_op jit(solution)/shard_map/ppermute | solution.py:24
  635.7 34.0 %copy-start.14 = (s32[6]{0:T(128)S(1)}, s32[6]{0:T(128)}, u32[]{:S(2)}) copy-start(s32[6]{0:T(128)} %copy-done.13) | copy-start | bytes 76
  635.7 34.0 %copy-start.16 = (pred[6]{0:T(512)(128)(4,1)S(1)}, pred[6]{0:T(512)(128)(4,1)}, u32[]{:S(2)}) copy-start(pred[6]{0:T(512)(128)(4,1)} %copy-done.15) | copy-start | bytes 22
  964.5 32.5 %collective-permute-start.2 = (bf16[128,6,64]{0,2,1:T(8,128)(2,1)}, bf16[128,6,64]{0,2,1:T(8,128)(2,1)}, u32[]{:S(2)}, u32[]{:S(2)}) collective-permute-start(bf16[128,6,64]{0,2,1:T(8,128)(2,1)} %get-tuple-element.20), channel_id=1, source_target_pairs={{0,2},{2,0},{4,6},{6,4},{8,10},{10,8},{12,14},{14,12},{16,18},{18,... | collective-permute-start | bytes 294920 | tf_op jit(solution)/shard_map/ppermute | solution.py:24
  964.6 15.6 %collective-permute-start.14 = (bf16[32,6,64]{2,0,1:T(8,128)(2,1)S(1)}, bf16[32,6,64]{2,0,1:T(8,128)(2,1)S(1)}, u32[]{:S(2)}, u32[]{:S(2)}) collective-permute-start(bf16[32,6,64]{2,0,1:T(8,128)(2,1)S(1)} %get-tuple-element.11), channel_id=1, source_target_pairs={{0,2},{2,0},{4,6},{6,4},{8,10},{10,8},{12,14},{14,12},{16,18},{18,... | collective-permute-start | bytes 73736 | tf_op jit(solution)/shard_map/ppermute | solution.py:24
  971.2 47.2 %all-to-all-start.1 = ((bf16[128,2,1536]{2,1,0:T(2,128)(2,1)}), bf16[128,2,1536]{2,1,0:T(2,128)(2,1)S(1)}, u32[]{:S(2)}, u32[]{:S(2)}) async-start(bf16[128,2,1536]{2,1,0:T(2,128)(2,1)} %reshape.335), calls=%async_computation.1 | async-start | bytes 1572864 | tf_op jit(solution)/shard_map/all_to_all | solution.py:143
  977.4 180.9 %reduce-scatter.4.cloned.1.call-start = ((), (), s32[]{:S(2)}) async-start(), calls=%async_computation.3 | async-start | bytes 294912
  977.4 21.5 %collective-permute-start.4 = (bf16[128,6,64]{0,2,1:T(8,128)(2,1)S(1)}, bf16[128,6,64]{0,2,1:T(8,128)(2,1)S(1)}, u32[]{:S(2)}, u32[]{:S(2)}) collective-permute-start(bf16[128,6,64]{0,2,1:T(8,128)(2,1)S(1)} %get-tuple-element.19), channel_id=1, source_target_pairs={{0,2},{2,0},{4,6},{6,4},{8,10},{10,8},{12,14},{14,12},{16,18},{18,... | collective-permute-start | bytes 294920 | tf_op jit(solution)/shard_map/ppermute | solution.py:24
  978.0 10.2 collective-permute-start.11
  980.2 12.2 %collective-permute-start.15 = (bf16[64,6,64]{2,0,1:T(8,128)(2,1)S(1)}, bf16[64,6,64]{2,0,1:T(8,128)(2,1)S(1)}, u32[]{:S(2)}, u32[]{:S(2)}) collective-permute-start(bf16[64,6,64]{2,0,1:T(8,128)(2,1)S(1)} %pad_maximum_fusion.7), channel_id=1, source_target_pairs={{0,4},{2,6},{4,0},{6,2},{8,12},{10,14},{12,8},{14,10},{16,20},{18,... | collective-permute-start | bytes 147464 | tf_op jit(solution)/shard_map/ppermute | solution.py:24
  988.2 12.9 %collective-permute-start.12 = (bf16[128,6,64]{2,0,1:T(8,128)(2,1)S(1)}, bf16[128,6,64]{2,0,1:T(8,128)(2,1)S(1)}, u32[]{:S(2)}, u32[]{:S(2)}) collective-permute-start(bf16[128,6,64]{2,0,1:T(8,128)(2,1)S(1)} %pad_maximum_fusion.4), channel_id=1, source_target_pairs={{0,8},{2,10},{4,12},{6,14},{8,0},{10,2},{12,4},{14,6},{16,24},{18,... | collective-permute-start | bytes 294920 | tf_op jit(solution)/shard_map/ppermute | solution.py:24
  992.4 10.7 collective-permute-start.16
  998.0 13.5 %collective-permute-start.3 = (bf16[256,6,64]{0,2,1:T(8,128)(2,1)S(1)}, bf16[256,6,64]{0,2,1:T(8,128)(2,1)S(1)}, u32[]{:S(2)}, u32[]{:S(2)}) collective-permute-start(bf16[256,6,64]{0,2,1:T(8,128)(2,1)S(1)} %pad_maximum_fusion.2), channel_id=1, source_target_pairs={{0,4},{2,6},{4,0},{6,2},{8,12},{10,14},{12,8},{14,10},{16,20},{18,... | collective-permute-start | bytes 589832 | tf_op jit(solution)/shard_map/ppermute | solution.py:24
  999.6 23.7 %collective-permute-start.5 = (bf16[256,6,64]{0,2,1:T(8,128)(2,1)}, bf16[256,6,64]{0,2,1:T(8,128)(2,1)}, u32[]{:S(2)}, u32[]{:S(2)}) collective-permute-start(bf16[256,6,64]{0,2,1:T(8,128)(2,1)} %pad_maximum_fusion.3), channel_id=1, source_target_pairs={{0,4},{2,6},{4,0},{6,2},{8,12},{10,14},{12,8},{14,10},{16,20},{18,... | collective-permute-start | bytes 589832 | tf_op jit(solution)/shard_map/ppermute | solution.py:24
  1001.2 11.7 %collective-permute-start.13 = (bf16[256,6,64]{2,0,1:T(8,128)(2,1)S(1)}, bf16[256,6,64]{2,0,1:T(8,128)(2,1)S(1)}, u32[]{:S(2)}, u32[]{:S(2)}) collective-permute-start(bf16[256,6,64]{2,0,1:T(8,128)(2,1)S(1)} %pad_maximum_fusion), channel_id=1, source_target_pairs={{0,16},{2,18},{4,20},{6,22},{8,24},{10,26},{12,28},{14,30},{16,0},... | collective-permute-start | bytes 589832 | tf_op jit(solution)/shard_map/ppermute | solution.py:24
  1003.2 10.3 collective-permute-start.17
  (17 other events, 89.7 us)
Sparse Core Ops, SparseCore 0:
  1026.8 131.3 reduce-scatter.3
